TPU v7x, 32 devices: a whole 2x2x4 slice. The times are simulated.
32 devices in a mesh: groups: 2 (over x), pages: 16 (over z, y, core).
Axes of the slice: x: 2, y: 2, z: 4, core: 2. Of those that a mesh axis runs over, the one named last changes fastest.
Arguments:
- queries: bfloat16 [2, 512, 8192], P(None, 'groups'), parts along dimension 1, may hold values from -14 to 14
- kv_cache: bfloat16 [256, 128, 2, 1024], P(('groups', 'pages')), parts along dimension 0, may hold values from -14 to 14
- w_out: bfloat16 [8192, 8192], P('pages'), may hold values from -0.0625 to 0.0625
- slot_page_before: int32 [256], P(('groups', 'pages')), parts along dimension 0, may hold values from -1 to 127, as said below
- slot_page_after: int32 [256], P(('groups', 'pages')), parts along dimension 0, may hold values from -1 to 127, as said below
- move_out: int32 [32, 4], P(('groups', 'pages')), parts along dimension 0, may hold values from -1 to 7, as said below
- move_in: int32 [32, 4], P(('groups', 'pages')), parts along dimension 0, may hold values from -1 to 7, as said below
- positions: int32 [2, 512], P(None, 'groups'), parts along dimension 1, may hold values from 0 to 16383, as said below
Outputs:
- attn_output: bfloat16 [2, 512, 8192], P(None, ('groups', 'pages')), parts along dimension 1
- cache_after: bfloat16 [256, 128, 2, 1024], P(('groups', 'pages')), parts along dimension 0
There are 2 independent parts, one for each index of `groups`. A program takes and returns all parts, laid end to end along the dimension named above; an argument that names none is the same for every part. Nothing has to cross between parts.
Inputs may be any that keep to these rules, and one draw needn't show every extreme that they name: `slot_page_before`: the logical page held by each slot; -1 marks a free slot; the live pages are the last ones of the sequence, numbered consecutively up to 127, each in exactly one slot; an owner's free slots are its last ones. `slot_page_after`: pages that are not sent keep their slot, each sent page sits in the slot that move_in names at its new owner, and a slot that sent its page is free. `move_out`: entry [j, o - 1] is a slot of owner j holding a live page, sent to owner (j + o) mod 16, or -1; the slots of one row differ; an owner sends at most one page to each of its next 4 owners. `move_in`: entry [j, o - 1] is a slot of owner j that is free before the moves, or -1, which it is exactly where move_out[(j - o) mod 16, o - 1] is -1; the slots of one row differ. Each row holds 256 consecutive positions; row 1 ends at the last position of the last live page; at most 256 positions lie between the end of row 0 and the start of row 1; all lie within the live pages.
All inputs are finite; a program needn't handle non-finite values.
Results may differ from a plain program's by a relative error of at most 0.0055.
Values may be sent and summed in bfloat16 or wider, within the bound.
No kernel may reach another device: no remote copies, remote signals or barrier semaphores. Data moves between devices by JAX's collectives and lax.ppermute only.
A program may use at most 192 MiB of HBM per device.

v0:
```python
import jax
import jax.numpy as jnp
from jax import lax
from jax.sharding import PartitionSpec as P

HEADS = 64
KV_HEADS = 8
HEAD_DIM = 128
D = 8192
PAGE_TOK = 128
BLOCK = 256
MOVE_WIN = 4
floor_score = -1e30


def passed_along(block, axis, distance):
    devices = range(lax.axis_size(axis))
    route = [((i - distance) % len(devices), i) for i in devices]
    return lax.ppermute(block, axis, route)


def block_partials(query_rows, cache_rows, slot_table, positions_row):
    key_count = cache_rows.shape[0] * PAGE_TOK
    head_group = HEADS // KV_HEADS
    key_rows = cache_rows[:, :, 0, :].reshape(key_count, KV_HEADS, HEAD_DIM)
    value_rows = cache_rows[:, :, 1, :].reshape(key_count, KV_HEADS, HEAD_DIM)
    key_pos = (
        slot_table[:, None] * PAGE_TOK + jnp.arange(PAGE_TOK, dtype=jnp.int32)[None, :]
    ).reshape(key_count)
    live_keys = jnp.repeat(slot_table >= 0, PAGE_TOK)
    sub_rows = min(64, BLOCK)
    score_scale = HEAD_DIM ** (-0.5)
    queries_in = query_rows.reshape(BLOCK // sub_rows, sub_rows, KV_HEADS, head_group, HEAD_DIM)
    places = positions_row.reshape(BLOCK // sub_rows, sub_rows)

    def one_block(inputs):
        query_block, query_pos = inputs
        scores = (
            jnp.einsum("qhgd,khd->qhgk", query_block, key_rows, preferred_element_type=jnp.float32)
            * score_scale
        )
        visible = (live_keys[None, :] & (key_pos[None, :] <= query_pos[:, None]))[:, None, None, :]
        scores = jnp.where(visible, scores, floor_score)
        row_max = jnp.max(scores, axis=-1)
        weights = jnp.where(visible, jnp.exp(scores - row_max[..., None]), 0.0).astype(jnp.bfloat16)
        row_sum = jnp.sum(weights, axis=-1, dtype=jnp.float32)
        mixed_rows = jnp.einsum(
            "qhgk,khd->qhgd", weights, value_rows, preferred_element_type=jnp.float32
        )
        return (
            mixed_rows.reshape(sub_rows, HEADS * HEAD_DIM),
            row_max.reshape(sub_rows, HEADS),
            row_sum.reshape(sub_rows, HEADS),
        )

    mixed_rows, row_max, row_sum = lax.map(one_block, (queries_in, places))
    return (
        mixed_rows.reshape(BLOCK, HEADS * HEAD_DIM),
        row_max.reshape(BLOCK, HEADS),
        row_sum.reshape(BLOCK, HEADS),
    )


def combine_parts(part_out, part_max, part_sum):
    sources, item_count, head_count = part_max.shape
    part_out = part_out.reshape(sources, item_count, head_count, HEAD_DIM)
    overall = jnp.max(part_max, axis=0)
    factor = jnp.exp(part_max - overall[None])
    weighted = jnp.sum(factor[..., None] * part_out, axis=0)
    normalizer = jnp.sum(factor * part_sum, axis=0)
    return (
        (weighted / normalizer[..., None])
        .reshape(item_count, head_count * HEAD_DIM)
        .astype(jnp.bfloat16)
    )


def migrate_pages(kv_cache, slot_page_after, move_out, move_in):
    slot_ids = jnp.arange(kv_cache.shape[0], dtype=jnp.int32)
    arranged = jnp.where(
        (slot_page_after >= 0)[:, None, None, None], kv_cache, jnp.zeros((), kv_cache.dtype)
    )
    outgoing = kv_cache[jnp.maximum(move_out[0], 0)]
    for offset in range(1, MOVE_WIN + 1):
        arrived = passed_along(outgoing[offset - 1], "pages", offset)
        landing = (slot_ids == move_in[0, offset - 1])[:, None, None, None]
        arranged = jnp.where(landing, arrived[None], arranged)
    return arranged


def local(
    queries, kv_cache, w_out, slot_page_before, slot_page_after, move_out, move_in, positions
):
    owners = lax.axis_size("pages")
    tok_rows = BLOCK // owners
    cache_after = migrate_pages(kv_cache, slot_page_after, move_out, move_in)
    results = []
    for block_index, (cache_rows, slot_table) in enumerate(
        ((kv_cache, slot_page_before), (cache_after, slot_page_after))
    ):
        part_out, part_max, part_sum = block_partials(
            queries[block_index], cache_rows, slot_table, positions[block_index]
        )
        merged = combine_parts(
            lax.all_to_all(
                part_out.reshape(1, owners, tok_rows, D),
                "pages",
                split_axis=1,
                concat_axis=0,
                tiled=True,
            )[:, 0],
            lax.all_to_all(
                part_max.reshape(1, owners, tok_rows, HEADS),
                "pages",
                split_axis=1,
                concat_axis=0,
                tiled=True,
            )[:, 0],
            lax.all_to_all(
                part_sum.reshape(1, owners, tok_rows, HEADS),
                "pages",
                split_axis=1,
                concat_axis=0,
                tiled=True,
            )[:, 0],
        )
        attended = lax.all_to_all(merged, "pages", split_axis=1, concat_axis=0, tiled=True)
        results.append(
            lax.psum_scatter(
                jnp.dot(attended, w_out, preferred_element_type=jnp.float32),
                "pages",
                scatter_dimension=0,
                tiled=True,
            ).astype(jnp.bfloat16)
        )
    return (jnp.stack(results), cache_after)


def solution(mesh):
    in_specs = (
        P(None, "groups", None),
        P(("groups", "pages"), None, None, None),
        P("pages", None),
        P(("groups", "pages")),
        P(("groups", "pages")),
        P(("groups", "pages"), None),
        P(("groups", "pages"), None),
        P(None, "groups"),
    )
    out_specs = (P(None, ("groups", "pages"), None), P(("groups", "pages"), None, None, None))
    return jax.shard_map(local, mesh=mesh, in_specs=in_specs, out_specs=out_specs, check_vma=False)
```

profile of v0, /device:TPU:0, one launch (start us, length us, event | category | flops | bytes accessed | tf_op | source)
XLA Modules:
  0.0 817.3 jit_solution(12786084088419435648)
XLA Ops:
  7.8 7.1 gather_fusion
  23.3 18.6 %slice_reduce_fusion.2 = (bf16[8,128,1024]{2,1,0:T(8,128)(2,1)S(1)}, bf16[8,128,1024]{2,1,0:T(8,128)(2,1)}) fusion(bf16[8,128,2,1024]{3,2,1,0:T(2,128)(2,1)S(1)} %copy-done.2), kind=kLoop, calls=%fused_computation.59 | loop fusion | bytes 8388608 | tf_op jit(solution)/shard_map/slice | solution.py:26
  59.1 126.9 %while.30 = (s32[]{:T(128)}, f32[4,64,8192]{2,1,0:T(8,128)}, f32[4,64,64]{2,1,0:T(8,128)S(1)}, f32[4,64,64]{2,1,0:T(8,128)S(1)}, s32[4,64]{1,0:T(4,128)S(1)}, /*...) while((s32[]{:T(128)}, f32[4,64,8192]{2,1,0:T(8,128)}, ...), condition=%wide.region_3.4_spmd.clone, body=%wide.region_0.3_spmd.clone.sunk | while | flops 2210522112 | bytes 137965520 | solution.py:56
  65.2 5.7 copy-done
  70.9 6.1 convert_reduce_fusion.4
  77.4 8.9 %fusion.58 = f32[64,8,8,128]{3,2,0,1:T(8,128)S(1)} fusion(bf16[1024,8,128]{2,0,1:T(8,128)(2,1)} %get-tuple-element.508, f32[8,64,8,1024]{3,2,1,0:T(8,128)} %copy-done, f32[64,8,8]{2,0,1:T(8,128)S(1)} %get-tuple-element.429, pred[64,1024]{1,0:T(8,128)(4,1)S(1)} %compare_and_fusion.4), kind=kOutput, calls=%fused_computation.16.clone.1 | convolution fusion | flops 1094713344 | bytes 21053440 | tf_op jit(solution)/shard_map/while/body/eval_jaxpr/qhgk,khd->qhgd/dot_general | solution.py:47
  91.5 5.2 bitcast_reduce_fusion.6
  96.8 5.7 copy-done
  102.5 6.1 convert_reduce_fusion.4
  109.1 8.9 %fusion.58 = f32[64,8,8,128]{3,2,0,1:T(8,128)S(1)} fusion(bf16[1024,8,128]{2,0,1:T(8,128)(2,1)} %get-tuple-element.508, f32[8,64,8,1024]{3,2,1,0:T(8,128)} %copy-done, f32[64,8,8]{2,0,1:T(8,128)S(1)} %get-tuple-element.429, pred[64,1024]{1,0:T(8,128)(4,1)S(1)} %compare_and_fusion.4), kind=kOutput, calls=%fused_computation.16.clone.1 | convolution fusion | flops 1094713344 | bytes 21053440 | tf_op jit(solution)/shard_map/while/body/eval_jaxpr/qhgk,khd->qhgd/dot_general | solution.py:47
  128.4 5.7 copy-done
  134.1 6.1 convert_reduce_fusion.4
  140.6 8.9 %fusion.58 = f32[64,8,8,128]{3,2,0,1:T(8,128)S(1)} fusion(bf16[1024,8,128]{2,0,1:T(8,128)(2,1)} %get-tuple-element.508, f32[8,64,8,1024]{3,2,1,0:T(8,128)} %copy-done, f32[64,8,8]{2,0,1:T(8,128)S(1)} %get-tuple-element.429, pred[64,1024]{1,0:T(8,128)(4,1)S(1)} %compare_and_fusion.4), kind=kOutput, calls=%fused_computation.16.clone.1 | convolution fusion | flops 1094713344 | bytes 21053440 | tf_op jit(solution)/shard_map/while/body/eval_jaxpr/qhgk,khd->qhgd/dot_general | solution.py:47
  160.0 5.7 copy-done
  165.7 6.1 convert_reduce_fusion.4
  172.2 8.9 %fusion.58 = f32[64,8,8,128]{3,2,0,1:T(8,128)S(1)} fusion(bf16[1024,8,128]{2,0,1:T(8,128)(2,1)} %get-tuple-element.508, f32[8,64,8,1024]{3,2,1,0:T(8,128)} %copy-done, f32[64,8,8]{2,0,1:T(8,128)S(1)} %get-tuple-element.429, pred[64,1024]{1,0:T(8,128)(4,1)S(1)} %compare_and_fusion.4), kind=kOutput, calls=%fused_computation.16.clone.1 | convolution fusion | flops 1094713344 | bytes 21053440 | tf_op jit(solution)/shard_map/while/body/eval_jaxpr/qhgk,khd->qhgd/dot_general | solution.py:47
  193.3 5.5 all-to-all-done
  203.6 5.4 copy.84
  211.7 6.2 all-to-all-start.1
  223.3 9.4 %mul.54 = f32[1,16,16,8192]{3,2,0,1:T(8,128)} reshape(f32[16,16,64,128]{3,2,1,0:T(8,128)} %mul.53) | data formatting | bytes 16777216 | tf_op jit(solution)/shard_map/mul | solution.py:69
  233.1 9.4 %broadcast_select_fusion.4 = bf16[8,128,2,1024]{3,2,1,0:T(2,128)(2,1)S(1)} fusion(pred[8]{0:T(512)(128)(4,1)S(1)} %get-tuple-element.307, pred[8]{0:T(512)(128)(4,1)S(1)} %get-tuple-element.306, pred[8]{0:T(512)(128)(4,1)S(1)} %get-tuple-element.305, pred[8]{0:T(512)(128)(4,1)S(1)} %get-tuple-element.304, bf16[8,128,2,1024]{3,2,1,0:T(2,128)(2,1)} %param.13, ...), kind=kLoop, calls=%fused_computation.55 | loop fusion | flops 10485760 | bytes 10485800 | tf_op jit(solution)/shard_map/jit(_where)/select_n | solution.py:87
  242.5 18.6 %slice_reduce_fusion = (bf16[8,128,1024]{2,1,0:T(8,128)(2,1)S(1)}, bf16[8,128,1024]{2,1,0:T(8,128)(2,1)}) fusion(bf16[8,128,2,1024]{3,2,1,0:T(2,128)(2,1)S(1)} %broadcast_select_fusion.4), kind=kLoop, calls=%fused_computation.56 | loop fusion | bytes 8388608 | tf_op jit(solution)/shard_map/slice | solution.py:26
  271.4 126.6 %while.31 = (s32[]{:T(128)}, f32[4,64,8192]{2,1,0:T(8,128)}, f32[4,64,64]{2,1,0:T(8,128)S(1)}, f32[4,64,64]{2,1,0:T(8,128)S(1)}, s32[4,64]{1,0:T(4,128)S(1)}, /*...) while((s32[]{:T(128)}, f32[4,64,8192]{2,1,0:T(8,128)}, ...), condition=%wide.region_11.12_spmd.clone, body=%wide.region_8.11_spmd.clone.sunk | while | flops 2210522112 | bytes 137965520 | solution.py:56
  277.2 5.7 copy-done.1
  282.9 6.1 convert_reduce_fusion.5
  289.4 8.9 %fusion.62 = f32[64,8,8,128]{3,2,0,1:T(8,128)S(1)} fusion(bf16[1024,8,128]{2,0,1:T(8,128)(2,1)} %get-tuple-element.475, f32[8,64,8,1024]{3,2,1,0:T(8,128)} %copy-done.1, f32[64,8,8]{2,0,1:T(8,128)S(1)} %get-tuple-element.443, pred[64,1024]{1,0:T(8,128)(4,1)S(1)} %compare_and_fusion.5), kind=kOutput, calls=%fused_computation.38.clone.1 | convolution fusion | flops 1094713344 | bytes 21053440 | tf_op jit(solution)/shard_map/while/body/eval_jaxpr/qhgk,khd->qhgd/dot_general | solution.py:47
  303.5 5.2 bitcast_reduce_fusion.7
  308.8 5.7 copy-done.1
  314.5 6.1 convert_reduce_fusion.5
  321.0 8.9 %fusion.62 = f32[64,8,8,128]{3,2,0,1:T(8,128)S(1)} fusion(bf16[1024,8,128]{2,0,1:T(8,128)(2,1)} %get-tuple-element.475, f32[8,64,8,1024]{3,2,1,0:T(8,128)} %copy-done.1, f32[64,8,8]{2,0,1:T(8,128)S(1)} %get-tuple-element.443, pred[64,1024]{1,0:T(8,128)(4,1)S(1)} %compare_and_fusion.5), kind=kOutput, calls=%fused_computation.38.clone.1 | convolution fusion | flops 1094713344 | bytes 21053440 | tf_op jit(solution)/shard_map/while/body/eval_jaxpr/qhgk,khd->qhgd/dot_general | solution.py:47
  340.4 5.7 copy-done.1
  346.1 6.1 convert_reduce_fusion.5
  352.7 8.9 %fusion.62 = f32[64,8,8,128]{3,2,0,1:T(8,128)S(1)} fusion(bf16[1024,8,128]{2,0,1:T(8,128)(2,1)} %get-tuple-element.475, f32[8,64,8,1024]{3,2,1,0:T(8,128)} %copy-done.1, f32[64,8,8]{2,0,1:T(8,128)S(1)} %get-tuple-element.443, pred[64,1024]{1,0:T(8,128)(4,1)S(1)} %compare_and_fusion.5), kind=kOutput, calls=%fused_computation.38.clone.1 | convolution fusion | flops 1094713344 | bytes 21053440 | tf_op jit(solution)/shard_map/while/body/eval_jaxpr/qhgk,khd->qhgd/dot_general | solution.py:47
  372.0 5.7 copy-done.1
  377.7 6.1 convert_reduce_fusion.5
  384.2 8.9 %fusion.62 = f32[64,8,8,128]{3,2,0,1:T(8,128)S(1)} fusion(bf16[1024,8,128]{2,0,1:T(8,128)(2,1)} %get-tuple-element.475, f32[8,64,8,1024]{3,2,1,0:T(8,128)} %copy-done.1, f32[64,8,8]{2,0,1:T(8,128)S(1)} %get-tuple-element.443, pred[64,1024]{1,0:T(8,128)(4,1)S(1)} %compare_and_fusion.5), kind=kOutput, calls=%fused_computation.38.clone.1 | convolution fusion | flops 1094713344 | bytes 21053440 | tf_op jit(solution)/shard_map/while/body/eval_jaxpr/qhgk,khd->qhgd/dot_general | solution.py:47
  399.5 6.1 all-to-all-start.4
  405.6 6.6 multiply_reduce_fusion.1
  412.6 6.0 all-to-all-start.6
  418.8 6.6 all-to-all-done.6
  425.5 12.6 %all_to_all.86 = bf16[16,16,512]{2,0,1:T(8,128)(2,1)S(1)} all-to-all(bf16[16,16,512]{2,0,1:T(8,128)(2,1)S(1)} %copy.53), channel_id=1, replica_groups=mesh['groups'=2,'pages'=16] {'pages'}, dimensions={1} | all-to-all | bytes 524288 | tf_op jit(solution)/shard_map/all_to_all | solution.py:127
  442.9 9.0 %fusion.41 = f32[256,8192]{1,0:T(8,128)} fusion(bf16[256,512]{1,0:T(8,128)(2,1)S(1)} %bitcast.262, bf16[512,8192]{1,0:T(8,128)(2,1)} %param.14), kind=kOutput, calls=%fused_computation.96 | convolution fusion | flops 2147483648 | bytes 17039360 | tf_op jit(solution)/shard_map/dot_general | solution.py:130
  458.5 9.7 %mul.59 = f32[1,16,16,8192]{3,2,0,1:T(8,128)} reshape(f32[16,16,64,128]{3,2,1,0:T(8,128)} %mul.58) | data formatting | bytes 16777216 | tf_op jit(solution)/shard_map/mul | solution.py:69
  468.5 158.6 %all-to-all-done.5 = f32[1,16,16,8192]{3,2,0,1:T(8,128)} async-done(((f32[1,16,16,8192]{3,2,0,1:T(8,128)}), f32[1,16,16,8192]{3,2,0,1:T(8,128)}, u32[]{:S(2)}, u32[]{:S(2)}) %all-to-all-start.5) | async-done | bytes 8388640 | tf_op jit(solution)/shard_map/all_to_all | solution.py:105
  627.1 7.0 multiply_reduce_fusion
  634.7 62.7 %all_to_all.87 = bf16[16,16,512]{2,0,1:T(8,128)(2,1)S(1)} all-to-all(bf16[16,16,512]{2,0,1:T(8,128)(2,1)S(1)} %copy.61), channel_id=1, replica_groups=mesh['groups'=2,'pages'=16] {'pages'}, dimensions={1} | all-to-all | bytes 524288 | tf_op jit(solution)/shard_map/all_to_all | solution.py:127
  697.4 9.0 %fusion.42 = f32[256,8192]{1,0:T(8,128)} fusion(bf16[256,512]{1,0:T(8,128)(2,1)S(1)} %bitcast.263, bf16[512,8192]{1,0:T(8,128)(2,1)} %param.14), kind=kOutput, calls=%fused_computation.97 | convolution fusion | flops 2147483648 | bytes 17039360 | tf_op jit(solution)/shard_map/dot_general | solution.py:130
  707.5 100.7 %reduce-scatter.5.cloned.1.call-done = f32[16,8192]{1,0:T(8,128)} async-done(((f32[256,8192]{1,0:T(8,128)}), f32[16,8192]{1,0:T(8,128)}) %reduce-scatter.5.cloned.1.call-update) | async-done | bytes 524304 | tf_op jit(solution)/shard_map/reduce_scatter | solution.py:129
  (204 shorter events, 149.9 us)
Async XLA Ops:
  14.9 8.4 %copy-start.2 = (bf16[8,128,2,1024]{3,2,1,0:T(2,128)(2,1)S(1)}, bf16[8,128,2,1024]{3,2,1,0:T(2,128)(2,1)}, u32[]{:S(2)}) copy-start(bf16[8,128,2,1024]{3,2,1,0:T(2,128)(2,1)} %param.13) | copy-start | bytes 12582916
  14.9 27.0 %copy-start.7 = (s32[8]{0:T(128)S(1)}, s32[8]{0:T(128)}, u32[]{:S(2)}) copy-start(s32[8]{0:T(128)} %param.15) | copy-start | bytes 100
  17.3 215.7 %collective-permute-start = (bf16[128,2,1024]{2,1,0:T(2,128)(2,1)}, bf16[128,2,1024]{2,1,0:T(2,128)(2,1)}, u32[]{:S(2)}, u32[]{:S(2)}) collective-permute-start(bf16[128,2,1024]{2,1,0:T(2,128)(2,1)} %get-tuple-element.296), channel_id=1, source_target_pairs={{12,0},{13,1},{14,2},{15,3},{0,4},{1,5},{2,6},{3,7},{4,8},{5,9},{6... | collective-permute-start | bytes 1572872 | tf_op jit(solution)/shard_map/ppermute | solution.py:19
  20.4 212.7 %collective-permute-start.1 = (bf16[128,2,1024]{2,1,0:T(2,128)(2,1)}, bf16[128,2,1024]{2,1,0:T(2,128)(2,1)}, u32[]{:S(2)}, u32[]{:S(2)}) collective-permute-start(bf16[128,2,1024]{2,1,0:T(2,128)(2,1)} %get-tuple-element.298), channel_id=1, source_target_pairs={{13,0},{14,1},{15,2},{0,3},{1,4},{2,5},{3,6},{4,7},{5,8},{6,9},{7,... | collective-permute-start | bytes 1572872 | tf_op jit(solution)/shard_map/ppermute | solution.py:19
  21.0 212.0 %collective-permute-start.2 = (bf16[128,2,1024]{2,1,0:T(2,128)(2,1)}, bf16[128,2,1024]{2,1,0:T(2,128)(2,1)}, u32[]{:S(2)}, u32[]{:S(2)}) collective-permute-start(bf16[128,2,1024]{2,1,0:T(2,128)(2,1)} %get-tuple-element.297), channel_id=1, source_target_pairs={{14,0},{15,1},{0,2},{1,3},{2,4},{3,5},{4,6},{5,7},{6,8},{7,9},{8,1... | collective-permute-start | bytes 1572872 | tf_op jit(solution)/shard_map/ppermute | solution.py:19
  22.6 210.5 %collective-permute-start.3 = (bf16[128,2,1024]{2,1,0:T(2,128)(2,1)}, bf16[128,2,1024]{2,1,0:T(2,128)(2,1)}, u32[]{:S(2)}, u32[]{:S(2)}) collective-permute-start(bf16[128,2,1024]{2,1,0:T(2,128)(2,1)} %get-tuple-element.299), channel_id=1, source_target_pairs={{15,0},{0,1},{1,2},{2,3},{3,4},{4,5},{5,6},{6,7},{7,8},{8,9},{9,10... | collective-permute-start | bytes 1572872 | tf_op jit(solution)/shard_map/ppermute | solution.py:19
  41.9 5.1 copy-start.6
  47.0 3.1 copy-start.4
  59.1 132.8 %copy-start.8 = (s32[8]{0:T(128)S(1)}, s32[8]{0:T(128)}, u32[]{:S(2)}) copy-start(s32[8]{0:T(128)} %param.16) | copy-start | bytes 100
  59.1 133.6 %copy-start.5 = (s32[1,4]{1,0:T(1,128)S(1)}, s32[1,4]{1,0:T(1,128)}, u32[]{:S(2)}) copy-start(s32[1,4]{1,0:T(1,128)} %param.18) | copy-start | bytes 52
  65.2 5.7 copy-start
  96.8 5.7 copy-start
  128.3 5.7 copy-start
  160.0 5.7 copy-start
  186.8 12.0 %all-to-all-start = ((f32[16,1,1024]{2,1,0:T(1,128)}), f32[16,1,1024]{2,1,0:T(1,128)S(1)}, u32[]{:S(2)}, u32[]{:S(2)}) async-start(f32[16,1,1024]{2,1,0:T(1,128)} %reshape.268), calls=%async_computation | async-start | bytes 131072 | tf_op jit(solution)/shard_map/all_to_all | solution.py:112
  198.8 12.9 %all-to-all-start.2 = ((f32[16,1,1024]{2,1,0:T(1,128)}), f32[16,1,1024]{2,1,0:T(1,128)S(1)}, u32[]{:S(2)}, u32[]{:S(2)}) async-start(f32[16,1,1024]{2,1,0:T(1,128)} %reshape.270), calls=%async_computation.2 | async-start | bytes 131072 | tf_op jit(solution)/shard_map/all_to_all | solution.py:119
  211.7 187.9 %all-to-all-start.1 = ((f32[1,16,16,8192]{3,2,0,1:T(8,128)}), f32[1,16,16,8192]{3,2,0,1:T(8,128)}, u32[]{:S(2)}, u32[]{:S(2)}) async-start(f32[1,16,16,8192]{3,2,0,1:T(8,128)} %bitcast.245), calls=%async_computation.1 | async-start | bytes 16777216 | tf_op jit(solution)/shard_map/all_to_all | solution.py:105
  242.5 20.8 %copy-start.3 = (bf16[8,128,2,1024]{3,2,1,0:T(2,128)(2,1)}, bf16[8,128,2,1024]{3,2,1,0:T(2,128)(2,1)S(1)}, u32[]{:S(2)}) copy-start(bf16[8,128,2,1024]{3,2,1,0:T(2,128)(2,1)S(1)} %broadcast_select_fusion.4) | copy-start | bytes 12582916
  277.2 5.7 copy-start.1
  308.8 5.7 copy-start.1
  340.4 5.7 copy-start.1
  372.0 5.7 copy-start.1
  399.5 13.0 %all-to-all-start.4 = ((f32[16,1,1024]{2,1,0:T(1,128)}), f32[16,1,1024]{2,1,0:T(1,128)S(1)}, u32[]{:S(2)}, u32[]{:S(2)}) async-start(f32[16,1,1024]{2,1,0:T(1,128)} %reshape.264), calls=%async_computation.5 | async-start | bytes 131072 | tf_op jit(solution)/shard_map/all_to_all | solution.py:112
  412.6 12.9 %all-to-all-start.6 = ((f32[16,1,1024]{2,1,0:T(1,128)}), f32[16,1,1024]{2,1,0:T(1,128)S(1)}, u32[]{:S(2)}, u32[]{:S(2)}) async-start(f32[16,1,1024]{2,1,0:T(1,128)} %reshape.266), calls=%async_computation.7 | async-start | bytes 131072 | tf_op jit(solution)/shard_map/all_to_all | solution.py:119
  438.1 189.1 %all-to-all-start.5 = ((f32[1,16,16,8192]{3,2,0,1:T(8,128)}), f32[1,16,16,8192]{3,2,0,1:T(8,128)}, u32[]{:S(2)}, u32[]{:S(2)}) async-start(f32[1,16,16,8192]{3,2,0,1:T(8,128)} %bitcast.244), calls=%async_computation.6 | async-start | bytes 16777216 | tf_op jit(solution)/shard_map/all_to_all | solution.py:105
  442.9 263.6 %reduce-scatter.3.cloned.1.call-start = ((), (), s32[]{:S(2)}) async-start(), calls=%async_computation.10 | async-start | bytes 8912896 | tf_op jit(solution)/shard_map/reduce_scatter | solution.py:129
  451.9 356.3 %reduce-scatter.5.cloned.1.call-start = ((), (), s32[]{:S(2)}) async-start(), calls=%async_computation.11 | async-start | bytes 8912896 | tf_op jit(solution)/shard_map/reduce_scatter | solution.py:129
Sparse Core Ops, SparseCore 0:
  452.0 206.1 reduce-scatter.2
  706.5 101.6 reduce-scatter.4
where the time goes:
time: 826 us; the launch traced here: 817 us
  waiting for transfers between devices  271 us (33%)
  local copies, waits for them, and re-layouts  203 us (25%)
  matrix products  131 us (16%)
  other arithmetic  82.8 us (10%)
  blocking collectives  75.3 us (9%)
  starting transfers between devices  37.8 us (5%)
  between operations  14.7 us (2%)
    all_to_all x2, waiting for transfers between devices, local(): lax.all_to_all(part_out.reshape(1, owners, tok_rows, D), 'pages', split_a...  159 us
    reduce_scatter x2, waiting for transfers between devices, local(): lax.psum_scatter(jnp.dot(attended, w_out, preferred_element_type=jnp.floa...  101 us
    all_to_all x2, blocking collectives, local(): lax.all_to_all(merged, 'pages', split_axis=1, concat_axis=0, tiled=True)  75.3 us
    dot_general x8, matrix products, one_block(): jnp.einsum('qhgk,khd->qhgd', weights, value_rows, preferred_element_type=...  71.5 us
    reduce_sum x8, other arithmetic, one_block(): row_sum = jnp.sum(weights, axis=-1, dtype=jnp.float32)  49 us
    while x16, local copies, waits for them, and re-layouts  45.6 us
    dot_general x8, matrix products, one_block(): jnp.einsum('qhgd,khd->qhgk', query_block, key_rows, preferred_element_typ...  41.9 us
    slice x2, local copies, waits for them, and re-layouts, block_partials(): value_rows = cache_rows[:, :, 1, :].reshape(key_count, KV_HEADS, HEAD_DIM)  37.2 us
  transfers between devices with their start and end apart: 12, of which 4 were waited for; matrix products, arithmetic and copies ran while one was open for 44% of the time, Pallas kernels for 0%

commit v1 on v0

--- a/solution.py
+++ b/solution.py
@@ -11,6 +11,29 @@
 BLOCK = 256
 MOVE_WIN = 4
 floor_score = -1e30
+
+
+def in_blocks(array, dim, size):
+    shape = array.shape
+    parts = array.reshape(*shape[:dim], size, shape[dim] // size, *shape[dim + 1 :])
+    return jnp.moveaxis(parts, dim, 0)
+
+
+def in_order(tiles, dim):
+    tiles = jnp.moveaxis(tiles, 0, dim)
+    lengths = tiles.shape
+    return tiles.reshape(*lengths[:dim], lengths[dim] * lengths[dim + 1], *lengths[dim + 2 :])
+
+
+def exchange_in_pairs(shard, axis, split_dim, concat_dim):
+    size, index = (lax.axis_size(axis), lax.axis_index(axis))
+    blocks = in_blocks(shard, split_dim, size)
+    finished = [blocks[index]]
+    for step in range(1, size):
+        sent = blocks[index ^ step]
+        finished.append(lax.ppermute(sent, axis, [(i, i ^ step) for i in range(size)]))
+    blocks = jnp.stack(finished)[index ^ jnp.arange(size)]
+    return in_order(blocks, concat_dim)
 
 
 def passed_along(block, axis, distance):
@@ -102,13 +125,7 @@
             queries[block_index], cache_rows, slot_table, positions[block_index]
         )
         merged = combine_parts(
-            lax.all_to_all(
-                part_out.reshape(1, owners, tok_rows, D),
-                "pages",
-                split_axis=1,
-                concat_axis=0,
-                tiled=True,
-            )[:, 0],
+            exchange_in_pairs(part_out.reshape(1, owners, tok_rows, D), "pages", 1, 0)[:, 0],
             lax.all_to_all(
                 part_max.reshape(1, owners, tok_rows, HEADS),
                 "pages",

time: 826 us -> 1100 us (1.33)
  starting transfers between devices: 37.8 us -> 163 us
  waiting for transfers between devices: 271 us -> 387 us
  local copies, waits for them, and re-layouts: 203 us -> 247 us
    ppermute x0 -> x30, waiting for transfers between devices: none -> 272 us  [exchange_in_pairs(): lax.ppermute(sent, axis, [(i, i ^ step) for i in range(size)])]
    all_to_all x2 -> x1, waiting for transfers between devices: 159 us -> 0.01 us  [local(): lax.all_to_all(merged, 'pages', split_axis=1, concat_axis=0, tiled=True)]
    ppermute x0 -> x30, starting transfers between devices: none -> 47.6 us  [exchange_in_pairs(): lax.ppermute(sent, axis, [(i, i ^ step) for i in range(size)])]
    ppermute x4, starting transfers between devices: 5.98 us -> 51.3 us  [passed_along(): return lax.ppermute(block, axis, route)]
    unnamed x35 -> x75, local copies, waits for them, and re-layouts: 28.4 us -> 69.7 us
    all_to_all x2, starting transfers between devices: 11.2 us -> 51.5 us  [local(): lax.all_to_all(part_max.reshape(1, owners, tok_rows, HEADS), 'pages', spl...]
    mul x4 -> x0, local copies, waits for them, and re-layouts: 28.6 us -> none  [combine_parts(): weighted = jnp.sum(factor[..., None] * part_out, axis=0)]
    gather x0 -> x2, local copies, waits for them, and re-layouts: none -> 15.5 us  [exchange_in_pairs(): blocks = jnp.stack(finished)[index ^ jnp.arange(size)]]
  transfers between devices with their start and end apart: 12 -> 41, of which waited for: 4 -> 14; matrix products, arithmetic and copies ran while one was open for 44% -> 11% of each run, Pallas kernels for 0% -> 0%
where the time goes in v1:
time: 1100 us
  waiting for transfers between devices  387 us (35%)
  local copies, waits for them, and re-layouts  247 us (22%)
  starting transfers between devices  163 us (15%)
  matrix products  131 us (12%)
  other arithmetic  79 us (7%)
  blocking collectives  72 us (7%)
  between operations  14.7 us (1%)
    ppermute x30, waiting for transfers between devices, exchange_in_pairs(): lax.ppermute(sent, axis, [(i, i ^ step) for i in range(size)])  272 us
    reduce_scatter x2, waiting for transfers between devices, local(): lax.psum_scatter(jnp.dot(attended, w_out, preferred_element_type=jnp.floa...  101 us
    all_to_all x1, blocking collectives, local(): lax.all_to_all(merged, 'pages', split_axis=1, concat_axis=0, tiled=True)  72 us
    dot_general x8, matrix products, one_block(): jnp.einsum('qhgk,khd->qhgd', weights, value_rows, preferred_element_type=...  71.5 us
    unnamed x75, local copies, waits for them, and re-layouts  69.7 us
    all_to_all x2, starting transfers between devices, local(): lax.all_to_all(part_max.reshape(1, owners, tok_rows, HEADS), 'pages', spl...  51.5 us
    ppermute x4, starting transfers between devices, passed_along(): return lax.ppermute(block, axis, route)  51.3 us
    reduce_sum x8, other arithmetic, one_block(): row_sum = jnp.sum(weights, axis=-1, dtype=jnp.float32)  49 us
  transfers between devices with their start and end apart: 41, of which 14 were waited for; matrix products, arithmetic and copies ran while one was open for 11% of the time, Pallas kernels for 0%

profile of v1, /device:TPU:0, one launch (start us, length us, event | category | flops | bytes accessed | tf_op | source)
XLA Modules:
  0.0 1095.7 jit_solution(14638407864464385658)
XLA Ops:
  16.8 18.6 %slice_reduce_fusion.2 = (bf16[8,128,1024]{2,1,0:T(8,128)(2,1)S(1)}, bf16[8,128,1024]{2,1,0:T(8,128)(2,1)}) fusion(bf16[8,128,2,1024]{3,2,1,0:T(2,128)(2,1)S(1)} %copy-done.2), kind=kLoop, calls=%fused_computation.63 | loop fusion | bytes 8388608 | tf_op jit(solution)/shard_map/slice | solution.py:49
  46.0 126.8 %while.30 = (s32[]{:T(128)}, f32[4,64,8192]{2,1,0:T(8,128)}, f32[4,64,64]{2,1,0:T(8,128)S(1)}, f32[4,64,64]{2,1,0:T(8,128)S(1)}, s32[4,64]{1,0:T(4,128)S(1)}, /*...) while((s32[]{:T(128)}, f32[4,64,8192]{2,1,0:T(8,128)}, ...), condition=%wide.region_3.4_spmd.clone, body=%wide.region_0.3_spmd.clone.sunk | while | flops 2210522112 | bytes 137965520 | solution.py:79
  51.7 5.7 copy-done
  57.4 6.1 convert_reduce_fusion.4
  64.0 8.9 fusion.59
  83.3 5.7 copy-done
  89.1 6.1 convert_reduce_fusion.4
  95.6 8.9 fusion.59
  120.7 6.1 convert_reduce_fusion.4
  127.2 8.9 fusion.59
  152.3 6.1 convert_reduce_fusion.4
  158.9 8.9 fusion.59
  172.7 6.7 dynamic-slice_bitcast_fusion.15
  185.2 6.1 all-to-all-start
  192.0 7.1 gather_fusion.1
  204.8 7.7 all-to-all-done
  241.9 16.2 %collective-permute-done.5 = f32[1,1,16,8192]{3,2,1,0:T(8,128)S(1)} collective-permute-done((f32[1,1,16,8192]{3,2,1,0:T(8,128)}, f32[1,1,16,8192]{3,2,1,0:T(8,128)S(1)}, u32[]{:S(2)}, u32[]{:S(2)}) %collective-permute-start.5) | collective-permute-done | bytes 524320 | tf_op jit(solution)/shard_map/ppermute | solution.py:34
  259.0 9.2 collective-permute-done.6
  273.8 51.8 %collective-permute-done.8 = f32[1,1,16,8192]{3,2,1,0:T(8,128)S(1)} collective-permute-done((f32[1,1,16,8192]{3,2,1,0:T(8,128)}, f32[1,1,16,8192]{3,2,1,0:T(8,128)S(1)}, u32[]{:S(2)}, u32[]{:S(2)}) %collective-permute-start.8) | collective-permute-done | bytes 524320 | tf_op jit(solution)/shard_map/ppermute | solution.py:34
  331.2 18.9 %collective-permute-done.9 = f32[1,1,16,8192]{3,2,1,0:T(8,128)S(1)} collective-permute-done((f32[1,1,16,8192]{3,2,1,0:T(8,128)}, f32[1,1,16,8192]{3,2,1,0:T(8,128)S(1)}, u32[]{:S(2)}, u32[]{:S(2)}) %collective-permute-start.9) | collective-permute-done | bytes 524320 | tf_op jit(solution)/shard_map/ppermute | solution.py:34
  353.4 18.6 %collective-permute-done.10 = f32[1,1,16,8192]{3,2,1,0:T(8,128)S(1)} collective-permute-done((f32[1,1,16,8192]{3,2,1,0:T(8,128)}, f32[1,1,16,8192]{3,2,1,0:T(8,128)S(1)}, u32[]{:S(2)}, u32[]{:S(2)}) %collective-permute-start.10) | collective-permute-done | bytes 524320 | tf_op jit(solution)/shard_map/ppermute | solution.py:34
  374.3 26.9 %collective-permute-start.17 = (bf16[128,2,1024]{2,1,0:T(2,128)(2,1)}, bf16[128,2,1024]{2,1,0:T(2,128)(2,1)S(1)}, u32[]{:S(2)}, u32[]{:S(2)}) collective-permute-start(bf16[128,2,1024]{2,1,0:T(2,128)(2,1)} %get-tuple-element.329), channel_id=1, source_target_pairs={{14,0},{15,1},{0,2},{1,3},{2,4},{3,5},{4,6},{5,7},{6,8},{7,9},{8,1... | collective-permute-start | bytes 1572872 | tf_op jit(solution)/shard_map/ppermute | solution.py:42
  402.0 23.7 %collective-permute-start.18 = (bf16[128,2,1024]{2,1,0:T(2,128)(2,1)}, bf16[128,2,1024]{2,1,0:T(2,128)(2,1)S(1)}, u32[]{:S(2)}, u32[]{:S(2)}) collective-permute-start(bf16[128,2,1024]{2,1,0:T(2,128)(2,1)} %get-tuple-element.331), channel_id=1, source_target_pairs={{15,0},{0,1},{1,2},{2,3},{3,4},{4,5},{5,6},{6,7},{7,8},{8,9},{9,10... | collective-permute-start | bytes 1572872 | tf_op jit(solution)/shard_map/ppermute | solution.py:42
  427.4 7.7 gather_fusion
  435.2 8.4 copy.83
  443.6 8.9 broadcast_select_fusion.4
  452.5 18.6 %slice_reduce_fusion = (bf16[8,128,1024]{2,1,0:T(8,128)(2,1)S(1)}, bf16[8,128,1024]{2,1,0:T(8,128)(2,1)}) fusion(bf16[8,128,2,1024]{3,2,1,0:T(2,128)(2,1)S(1)} %broadcast_select_fusion.4), kind=kLoop, calls=%fused_computation.60 | loop fusion | bytes 8388608 | tf_op jit(solution)/shard_map/slice | solution.py:49
  481.5 127.0 %while.31 = (s32[]{:T(128)}, f32[4,64,8192]{2,1,0:T(8,128)}, f32[4,64,64]{2,1,0:T(8,128)S(1)}, f32[4,64,64]{2,1,0:T(8,128)S(1)}, s32[4,64]{1,0:T(4,128)S(1)}, /*...) while((s32[]{:T(128)}, f32[4,64,8192]{2,1,0:T(8,128)}, ...), condition=%wide.region_11.12_spmd.clone, body=%wide.region_8.11_spmd.clone.sunk | while | flops 2210522112 | bytes 137965520 | solution.py:79
  493.2 6.1 convert_reduce_fusion.5
  499.8 8.9 fusion.63
  524.9 6.1 convert_reduce_fusion.5
  531.5 8.9 fusion.63
  556.5 6.1 convert_reduce_fusion.5
  563.1 8.9 fusion.63
  588.2 6.1 convert_reduce_fusion.5
  594.7 8.9 fusion.63
  609.3 45.4 %all-to-all-start.3 = ((f32[16,1,1024]{2,1,0:T(1,128)}), f32[16,1,1024]{2,1,0:T(1,128)S(1)}, u32[]{:S(2)}, u32[]{:S(2)}) async-start(f32[16,1,1024]{2,1,0:T(1,128)} %reshape.320), calls=%async_computation.4 | async-start | bytes 131072 | tf_op jit(solution)/shard_map/all_to_all | solution.py:129
  677.4 6.8 dynamic-slice_bitcast_fusion
  689.9 9.0 fusion.42
  703.3 6.2 collective-permute-done.21
  718.7 44.3 %collective-permute-done.24 = f32[1,1,16,8192]{3,2,1,0:T(8,128)S(1)} collective-permute-done((f32[1,1,16,8192]{3,2,1,0:T(8,128)}, f32[1,1,16,8192]{3,2,1,0:T(8,128)S(1)}, u32[]{:S(2)}, u32[]{:S(2)}) %collective-permute-start.24) | collective-permute-done | bytes 524320 | tf_op jit(solution)/shard_map/ppermute | solution.py:34
  763.8 14.5 %collective-permute-done.25 = f32[1,1,16,8192]{3,2,1,0:T(8,128)S(1)} collective-permute-done((f32[1,1,16,8192]{3,2,1,0:T(8,128)}, f32[1,1,16,8192]{3,2,1,0:T(8,128)S(1)}, u32[]{:S(2)}, u32[]{:S(2)}) %collective-permute-start.25) | collective-permute-done | bytes 524320 | tf_op jit(solution)/shard_map/ppermute | solution.py:34
  786.2 72.2 %collective-permute-done.28 = f32[1,1,16,8192]{3,2,1,0:T(8,128)S(1)} collective-permute-done((f32[1,1,16,8192]{3,2,1,0:T(8,128)}, f32[1,1,16,8192]{3,2,1,0:T(8,128)S(1)}, u32[]{:S(2)}, u32[]{:S(2)}) %collective-permute-start.28) | collective-permute-done | bytes 524320 | tf_op jit(solution)/shard_map/ppermute | solution.py:34
  863.3 20.3 %collective-permute-done.29 = f32[1,1,16,8192]{3,2,1,0:T(8,128)S(1)} collective-permute-done((f32[1,1,16,8192]{3,2,1,0:T(8,128)}, f32[1,1,16,8192]{3,2,1,0:T(8,128)S(1)}, u32[]{:S(2)}, u32[]{:S(2)}) %collective-permute-start.29) | collective-permute-done | bytes 524320 | tf_op jit(solution)/shard_map/ppermute | solution.py:34
  887.9 7.8 gather_fusion.2
  903.8 72.0 %all_to_all.68 = bf16[16,16,512]{2,0,1:T(8,128)(2,1)S(1)} all-to-all(bf16[16,16,512]{2,0,1:T(8,128)(2,1)S(1)} %copy.61), channel_id=1, replica_groups=mesh['groups'=2,'pages'=16] {'pages'}, dimensions={1} | all-to-all | bytes 524288 | tf_op jit(solution)/shard_map/all_to_all | solution.py:144
  975.8 9.1 fusion.43
  986.0 100.7 %reduce-scatter.5.cloned.1.call-done = f32[16,8192]{1,0:T(8,128)} async-done(((f32[256,8192]{1,0:T(8,128)}), f32[16,8192]{1,0:T(8,128)}) %reduce-scatter.5.cloned.1.call-update) | async-done | bytes 524304 | tf_op jit(solution)/shard_map/reduce_scatter | solution.py:146
  (303 shorter events, 284.5 us)
Async XLA Ops:
  179.4 46.1 %collective-permute-start = (f32[1,1,16,8192]{3,2,1,0:T(8,128)}, f32[1,1,16,8192]{3,2,1,0:T(8,128)}, u32[]{:S(2)}, u32[]{:S(2)}) collective-permute-start(f32[1,1,16,8192]{3,2,1,0:T(8,128)} %get-tuple-element.308), channel_id=1, source_target_pairs={{0,1},{1,0},{2,3},{3,2},{4,5},{5,4},{6,7},{7,6},{8,9},{9,8},{10,11... | collective-permute-start | bytes 1572872 | tf_op jit(solution)/shard_map/ppermute | solution.py:34
  180.0 50.2 %collective-permute-start.1 = (f32[1,1,16,8192]{3,2,1,0:T(8,128)}, f32[1,1,16,8192]{3,2,1,0:T(8,128)}, u32[]{:S(2)}, u32[]{:S(2)}) collective-permute-start(f32[1,1,16,8192]{3,2,1,0:T(8,128)} %get-tuple-element.307), channel_id=1, source_target_pairs={{0,2},{1,3},{2,0},{3,1},{4,6},{5,7},{6,4},{7,5},{8,10},{9,11},{10,... | collective-permute-start | bytes 1572872 | tf_op jit(solution)/shard_map/ppermute | solution.py:34
  182.6 49.5 %collective-permute-start.2 = (f32[1,1,16,8192]{3,2,1,0:T(8,128)}, f32[1,1,16,8192]{3,2,1,0:T(8,128)}, u32[]{:S(2)}, u32[]{:S(2)}) collective-permute-start(f32[1,1,16,8192]{3,2,1,0:T(8,128)} %get-tuple-element.306), channel_id=1, source_target_pairs={{0,3},{1,2},{2,1},{3,0},{4,7},{5,6},{6,5},{7,4},{8,11},{9,10},{10,... | collective-permute-start | bytes 1572872 | tf_op jit(solution)/shard_map/ppermute | solution.py:34
  182.6 53.8 %collective-permute-start.3 = (f32[1,1,16,8192]{3,2,1,0:T(8,128)}, f32[1,1,16,8192]{3,2,1,0:T(8,128)S(1)}, u32[]{:S(2)}, u32[]{:S(2)}) collective-permute-start(f32[1,1,16,8192]{3,2,1,0:T(8,128)} %get-tuple-element.305), channel_id=1, source_target_pairs={{0,4},{1,5},{2,6},{3,7},{4,0},{5,1},{6,2},{7,3},{8,12},{9,13},{10,... | collective-permute-start | bytes 1572872 | tf_op jit(solution)/shard_map/ppermute | solution.py:34
  184.4 53.1 %collective-permute-start.4 = (f32[1,1,16,8192]{3,2,1,0:T(8,128)}, f32[1,1,16,8192]{3,2,1,0:T(8,128)S(1)}, u32[]{:S(2)}, u32[]{:S(2)}) collective-permute-start(f32[1,1,16,8192]{3,2,1,0:T(8,128)} %get-tuple-element.304), channel_id=1, source_target_pairs={{0,5},{1,4},{2,7},{3,6},{4,1},{5,0},{6,3},{7,2},{8,13},{9,12},{10,... | collective-permute-start | bytes 1572872 | tf_op jit(solution)/shard_map/ppermute | solution.py:34
  185.2 27.4 %all-to-all-start = ((f32[16,1,1024]{2,1,0:T(1,128)}), f32[16,1,1024]{2,1,0:T(1,128)S(1)}, u32[]{:S(2)}, u32[]{:S(2)}) async-start(f32[16,1,1024]{2,1,0:T(1,128)} %reshape.324), calls=%async_computation | async-start | bytes 131072 | tf_op jit(solution)/shard_map/all_to_all | solution.py:129
  201.5 66.8 %copy-start.8 = (f32[1,1,16,8192]{3,2,1,0:T(8,128)S(1)}, f32[1,1,16,8192]{3,2,1,0:T(8,128)}, u32[]{:S(2)}) copy-start(f32[1,1,16,8192]{3,2,1,0:T(8,128)} %get-tuple-element.297) | copy-start | bytes 1572868
  212.5 10.8 all-to-all-start.1
  216.2 54.2 %copy-start.7 = (f32[1,1,16,8192]{3,2,1,0:T(8,128)S(1)}, f32[1,1,16,8192]{3,2,1,0:T(8,128)}, u32[]{:S(2)}) copy-start(f32[1,1,16,8192]{3,2,1,0:T(8,128)} %get-tuple-element.296) | copy-start | bytes 1572868
  216.3 109.4 %copy-start.6 = (f32[1,1,16,8192]{3,2,1,0:T(8,128)S(1)}, f32[1,1,16,8192]{3,2,1,0:T(8,128)}, u32[]{:S(2)}) copy-start(f32[1,1,16,8192]{3,2,1,0:T(8,128)} %get-tuple-element.295) | copy-start | bytes 1572868
  221.9 205.6 %copy-start.11 = (s32[1024]{0:T(1024)}, s32[1024]{0:T(1024)S(1)}, u32[]{:S(2)}) copy-start(s32[1024]{0:T(1024)S(1)} %pad_clamp_fusion.1) | copy-start | bytes 12292
  225.5 32.7 %collective-permute-start.5 = (f32[1,1,16,8192]{3,2,1,0:T(8,128)}, f32[1,1,16,8192]{3,2,1,0:T(8,128)S(1)}, u32[]{:S(2)}, u32[]{:S(2)}) collective-permute-start(f32[1,1,16,8192]{3,2,1,0:T(8,128)} %get-tuple-element.303), channel_id=1, source_target_pairs={{0,6},{1,7},{2,4},{3,5},{4,2},{5,3},{6,0},{7,1},{8,14},{9,15},{10,... | collective-permute-start | bytes 1572872 | tf_op jit(solution)/shard_map/ppermute | solution.py:34
  230.2 38.0 %collective-permute-start.6 = (f32[1,1,16,8192]{3,2,1,0:T(8,128)}, f32[1,1,16,8192]{3,2,1,0:T(8,128)S(1)}, u32[]{:S(2)}, u32[]{:S(2)}) collective-permute-start(f32[1,1,16,8192]{3,2,1,0:T(8,128)} %get-tuple-element.302), channel_id=1, source_target_pairs={{0,7},{1,6},{2,5},{3,4},{4,3},{5,2},{6,1},{7,0},{8,15},{9,14},{10,... | collective-permute-start | bytes 1572872 | tf_op jit(solution)/shard_map/ppermute | solution.py:34
  232.1 38.3 %collective-permute-start.7 = (f32[1,1,16,8192]{3,2,1,0:T(8,128)}, f32[1,1,16,8192]{3,2,1,0:T(8,128)S(1)}, u32[]{:S(2)}, u32[]{:S(2)}) collective-permute-start(f32[1,1,16,8192]{3,2,1,0:T(8,128)} %get-tuple-element.301), channel_id=1, source_target_pairs={{0,8},{1,9},{2,10},{3,11},{4,12},{5,13},{6,14},{7,15},{8,0},{9,1},... | collective-permute-start | bytes 1572872 | tf_op jit(solution)/shard_map/ppermute | solution.py:34
  236.4 89.2 %collective-permute-start.8 = (f32[1,1,16,8192]{3,2,1,0:T(8,128)}, f32[1,1,16,8192]{3,2,1,0:T(8,128)S(1)}, u32[]{:S(2)}, u32[]{:S(2)}) collective-permute-start(f32[1,1,16,8192]{3,2,1,0:T(8,128)} %get-tuple-element.300), channel_id=1, source_target_pairs={{0,9},{1,8},{2,11},{3,10},{4,13},{5,12},{6,15},{7,14},{8,1},{9,0},... | collective-permute-start | bytes 1572872 | tf_op jit(solution)/shard_map/ppermute | solution.py:34
  237.5 112.5 %collective-permute-start.9 = (f32[1,1,16,8192]{3,2,1,0:T(8,128)}, f32[1,1,16,8192]{3,2,1,0:T(8,128)S(1)}, u32[]{:S(2)}, u32[]{:S(2)}) collective-permute-start(f32[1,1,16,8192]{3,2,1,0:T(8,128)} %get-tuple-element.299), channel_id=1, source_target_pairs={{0,10},{1,11},{2,8},{3,9},{4,14},{5,15},{6,12},{7,13},{8,2},{9,3},... | collective-permute-start | bytes 1572872 | tf_op jit(solution)/shard_map/ppermute | solution.py:34
  258.2 113.8 %collective-permute-start.10 = (f32[1,1,16,8192]{3,2,1,0:T(8,128)}, f32[1,1,16,8192]{3,2,1,0:T(8,128)S(1)}, u32[]{:S(2)}, u32[]{:S(2)}) collective-permute-start(f32[1,1,16,8192]{3,2,1,0:T(8,128)} %get-tuple-element.298), channel_id=1, source_target_pairs={{0,11},{1,10},{2,9},{3,8},{4,15},{5,14},{6,13},{7,12},{8,3},{9,2},... | collective-permute-start | bytes 1572872 | tf_op jit(solution)/shard_map/ppermute | solution.py:34
  268.2 104.9 %collective-permute-start.11 = (f32[1,1,16,8192]{3,2,1,0:T(8,128)S(1)}, f32[1,1,16,8192]{3,2,1,0:T(8,128)S(1)}, u32[]{:S(2)}, u32[]{:S(2)}) collective-permute-start(f32[1,1,16,8192]{3,2,1,0:T(8,128)S(1)} %copy-done.8), channel_id=1, source_target_pairs={{0,12},{1,13},{2,14},{3,15},{4,8},{5,9},{6,10},{7,11},{8,4},{9,5},... | collective-permute-start | bytes 1572872 | tf_op jit(solution)/shard_map/ppermute | solution.py:34
  270.4 103.8 %collective-permute-start.12 = (f32[1,1,16,8192]{3,2,1,0:T(8,128)S(1)}, f32[1,1,16,8192]{3,2,1,0:T(8,128)S(1)}, u32[]{:S(2)}, u32[]{:S(2)}) collective-permute-start(f32[1,1,16,8192]{3,2,1,0:T(8,128)S(1)} %copy-done.7), channel_id=1, source_target_pairs={{0,13},{1,12},{2,15},{3,14},{4,9},{5,8},{6,11},{7,10},{8,5},{9,4},... | collective-permute-start | bytes 1572872 | tf_op jit(solution)/shard_map/ppermute | solution.py:34
  325.6 76.4 %collective-permute-start.13 = (f32[1,1,16,8192]{3,2,1,0:T(8,128)S(1)}, f32[1,1,16,8192]{3,2,1,0:T(8,128)S(1)}, u32[]{:S(2)}, u32[]{:S(2)}) collective-permute-start(f32[1,1,16,8192]{3,2,1,0:T(8,128)S(1)} %copy-done.6), channel_id=1, source_target_pairs={{0,14},{1,15},{2,12},{3,13},{4,10},{5,11},{6,8},{7,9},{8,6},{9,7},... | collective-permute-start | bytes 1572872 | tf_op jit(solution)/shard_map/ppermute | solution.py:34
  350.1 76.5 %collective-permute-start.14 = (f32[1,1,16,8192]{3,2,1,0:T(8,128)}, f32[1,1,16,8192]{3,2,1,0:T(8,128)S(1)}, u32[]{:S(2)}, u32[]{:S(2)}) collective-permute-start(f32[1,1,16,8192]{3,2,1,0:T(8,128)} %get-tuple-element.294), channel_id=1, source_target_pairs={{0,15},{1,14},{2,13},{3,12},{4,11},{5,10},{6,9},{7,8},{8,7},{9,6},... | collective-permute-start | bytes 1572872 | tf_op jit(solution)/shard_map/ppermute | solution.py:34
  371.9 71.6 %collective-permute-start.15 = (bf16[128,2,1024]{2,1,0:T(2,128)(2,1)}, bf16[128,2,1024]{2,1,0:T(2,128)(2,1)S(1)}, u32[]{:S(2)}, u32[]{:S(2)}) collective-permute-start(bf16[128,2,1024]{2,1,0:T(2,128)(2,1)} %get-tuple-element.328), channel_id=1, source_target_pairs={{12,0},{13,1},{14,2},{15,3},{0,4},{1,5},{2,6},{3,7},{4,8},{5,9},{6... | collective-permute-start | bytes 1572872 | tf_op jit(solution)/shard_map/ppermute | solution.py:42
  373.1 70.4 %collective-permute-start.16 = (bf16[128,2,1024]{2,1,0:T(2,128)(2,1)}, bf16[128,2,1024]{2,1,0:T(2,128)(2,1)S(1)}, u32[]{:S(2)}, u32[]{:S(2)}) collective-permute-start(bf16[128,2,1024]{2,1,0:T(2,128)(2,1)} %get-tuple-element.330), channel_id=1, source_target_pairs={{13,0},{14,1},{15,2},{0,3},{1,4},{2,5},{3,6},{4,7},{5,8},{6,9},{7,... | collective-permute-start | bytes 1572872 | tf_op jit(solution)/shard_map/ppermute | solution.py:42
  374.3 69.3 %collective-permute-start.17 = (bf16[128,2,1024]{2,1,0:T(2,128)(2,1)}, bf16[128,2,1024]{2,1,0:T(2,128)(2,1)S(1)}, u32[]{:S(2)}, u32[]{:S(2)}) collective-permute-start(bf16[128,2,1024]{2,1,0:T(2,128)(2,1)} %get-tuple-element.329), channel_id=1, source_target_pairs={{14,0},{15,1},{0,2},{1,3},{2,4},{3,5},{4,6},{5,7},{6,8},{7,9},{8,1... | collective-permute-start | bytes 1572872 | tf_op jit(solution)/shard_map/ppermute | solution.py:42
  402.0 41.5 %collective-permute-start.18 = (bf16[128,2,1024]{2,1,0:T(2,128)(2,1)}, bf16[128,2,1024]{2,1,0:T(2,128)(2,1)S(1)}, u32[]{:S(2)}, u32[]{:S(2)}) collective-permute-start(bf16[128,2,1024]{2,1,0:T(2,128)(2,1)} %get-tuple-element.331), channel_id=1, source_target_pairs={{15,0},{0,1},{1,2},{2,3},{3,4},{4,5},{5,6},{6,7},{7,8},{8,9},{9,10... | collective-permute-start | bytes 1572872 | tf_op jit(solution)/shard_map/ppermute | solution.py:42
  452.4 20.9 %copy-start.4 = (bf16[8,128,2,1024]{3,2,1,0:T(2,128)(2,1)}, bf16[8,128,2,1024]{3,2,1,0:T(2,128)(2,1)S(1)}, u32[]{:S(2)}) copy-start(bf16[8,128,2,1024]{3,2,1,0:T(2,128)(2,1)S(1)} %broadcast_select_fusion.4) | copy-start | bytes 12582916
  481.5 173.2 %copy-start.5 = (f32[16,16,64]{2,1,0:T(8,128)S(1)}, f32[16,16,64]{2,1,0:T(8,128)}, u32[]{:S(2)}) copy-start(f32[16,16,64]{2,1,0:T(8,128)} %get-tuple-element.283) | copy-start | bytes 196612
  608.5 58.3 %copy-start.9 = (f32[16,64]{1,0:T(8,128)S(1)}, f32[16,64]{1,0:T(8,128)}, u32[]{:S(2)}) copy-start(f32[16,64]{1,0:T(8,128)} %get-tuple-element.282) | copy-start | bytes 12292
  609.3 52.3 %all-to-all-start.3 = ((f32[16,1,1024]{2,1,0:T(1,128)}), f32[16,1,1024]{2,1,0:T(1,128)S(1)}, u32[]{:S(2)}, u32[]{:S(2)}) async-start(f32[16,1,1024]{2,1,0:T(1,128)} %reshape.320), calls=%async_computation.4 | async-start | bytes 131072 | tf_op jit(solution)/shard_map/all_to_all | solution.py:129
  661.6 12.1 %all-to-all-start.4 = ((f32[16,1,1024]{2,1,0:T(1,128)}), f32[16,1,1024]{2,1,0:T(1,128)S(1)}, u32[]{:S(2)}, u32[]{:S(2)}) async-start(f32[16,1,1024]{2,1,0:T(1,128)} %reshape.322), calls=%async_computation.5 | async-start | bytes 131072 | tf_op jit(solution)/shard_map/all_to_all | solution.py:136
  673.7 16.2 %all-to-all-start.2 = ((bf16[16,16,512]{2,0,1:T(8,128)(2,1)}), bf16[16,16,512]{2,0,1:T(8,128)(2,1)S(1)}, u32[]{:S(2)}, u32[]{:S(2)}) async-start(bf16[16,16,512]{2,0,1:T(8,128)(2,1)} %copy.53), calls=%async_computation.2 | async-start | bytes 524288 | tf_op jit(solution)/shard_map/all_to_all | solution.py:144
  677.2 307.7 %reduce-scatter.3.cloned.1.call-start = ((), (), s32[]{:S(2)}) async-start(), calls=%async_computation.8 | async-start | bytes 8912896 | tf_op jit(solution)/shard_map/reduce_scatter | solution.py:146
  684.2 14.7 %collective-permute-start.19 = (f32[1,1,16,8192]{3,2,1,0:T(8,128)}, f32[1,1,16,8192]{3,2,1,0:T(8,128)S(1)}, u32[]{:S(2)}, u32[]{:S(2)}) collective-permute-start(f32[1,1,16,8192]{3,2,1,0:T(8,128)} %get-tuple-element.326), channel_id=1, source_target_pairs={{0,1},{1,0},{2,3},{3,2},{4,5},{5,4},{6,7},{7,6},{8,9},{9,8},{10,11... | collective-permute-start | bytes 1572872 | tf_op jit(solution)/shard_map/ppermute | solution.py:34
  684.6 17.9 %collective-permute-start.20 = (f32[1,1,16,8192]{3,2,1,0:T(8,128)}, f32[1,1,16,8192]{3,2,1,0:T(8,128)S(1)}, u32[]{:S(2)}, u32[]{:S(2)}) collective-permute-start(f32[1,1,16,8192]{3,2,1,0:T(8,128)} %get-tuple-element.325), channel_id=1, source_target_pairs={{0,2},{1,3},{2,0},{3,1},{4,6},{5,7},{6,4},{7,5},{8,10},{9,11},{10,... | collective-permute-start | bytes 1572872 | tf_op jit(solution)/shard_map/ppermute | solution.py:34
  686.2 23.3 %collective-permute-start.21 = (f32[1,1,16,8192]{3,2,1,0:T(8,128)}, f32[1,1,16,8192]{3,2,1,0:T(8,128)S(1)}, u32[]{:S(2)}, u32[]{:S(2)}) collective-permute-start(f32[1,1,16,8192]{3,2,1,0:T(8,128)} %get-tuple-element.324), channel_id=1, source_target_pairs={{0,3},{1,2},{2,1},{3,0},{4,7},{5,6},{6,5},{7,4},{8,11},{9,10},{10,... | collective-permute-start | bytes 1572872 | tf_op jit(solution)/shard_map/ppermute | solution.py:34
  686.2 26.9 %collective-permute-start.22 = (f32[1,1,16,8192]{3,2,1,0:T(8,128)}, f32[1,1,16,8192]{3,2,1,0:T(8,128)S(1)}, u32[]{:S(2)}, u32[]{:S(2)}) collective-permute-start(f32[1,1,16,8192]{3,2,1,0:T(8,128)} %get-tuple-element.323), channel_id=1, source_target_pairs={{0,4},{1,5},{2,6},{3,7},{4,0},{5,1},{6,2},{7,3},{8,12},{9,13},{10,... | collective-permute-start | bytes 1572872 | tf_op jit(solution)/shard_map/ppermute | solution.py:34
  688.0 26.3 %collective-permute-start.23 = (f32[1,1,16,8192]{3,2,1,0:T(8,128)}, f32[1,1,16,8192]{3,2,1,0:T(8,128)S(1)}, u32[]{:S(2)}, u32[]{:S(2)}) collective-permute-start(f32[1,1,16,8192]{3,2,1,0:T(8,128)} %get-tuple-element.322), channel_id=1, source_target_pairs={{0,5},{1,4},{2,7},{3,6},{4,1},{5,0},{6,3},{7,2},{8,13},{9,12},{10,... | collective-permute-start | bytes 1572872 | tf_op jit(solution)/shard_map/ppermute | solution.py:34
  698.9 387.8 %reduce-scatter.5.cloned.1.call-start = ((), (), s32[]{:S(2)}) async-start(), calls=%async_computation.9 | async-start | bytes 8912896 | tf_op jit(solution)/shard_map/reduce_scatter | solution.py:146
  699.0 64.0 %collective-permute-start.24 = (f32[1,1,16,8192]{3,2,1,0:T(8,128)}, f32[1,1,16,8192]{3,2,1,0:T(8,128)S(1)}, u32[]{:S(2)}, u32[]{:S(2)}) collective-permute-start(f32[1,1,16,8192]{3,2,1,0:T(8,128)} %get-tuple-element.321), channel_id=1, source_target_pairs={{0,6},{1,7},{2,4},{3,5},{4,2},{5,3},{6,0},{7,1},{8,14},{9,15},{10,... | collective-permute-start | bytes 1572872 | tf_op jit(solution)/shard_map/ppermute | solution.py:34
  702.5 75.8 %collective-permute-start.25 = (f32[1,1,16,8192]{3,2,1,0:T(8,128)}, f32[1,1,16,8192]{3,2,1,0:T(8,128)S(1)}, u32[]{:S(2)}, u32[]{:S(2)}) collective-permute-start(f32[1,1,16,8192]{3,2,1,0:T(8,128)} %get-tuple-element.320), channel_id=1, source_target_pairs={{0,7},{1,6},{2,5},{3,4},{4,3},{5,2},{6,1},{7,0},{8,15},{9,14},{10,... | collective-permute-start | bytes 1572872 | tf_op jit(solution)/shard_map/ppermute | solution.py:34
  709.5 71.0 %collective-permute-start.26 = (f32[1,1,16,8192]{3,2,1,0:T(8,128)}, f32[1,1,16,8192]{3,2,1,0:T(8,128)S(1)}, u32[]{:S(2)}, u32[]{:S(2)}) collective-permute-start(f32[1,1,16,8192]{3,2,1,0:T(8,128)} %get-tuple-element.319), channel_id=1, source_target_pairs={{0,8},{1,9},{2,10},{3,11},{4,12},{5,13},{6,14},{7,15},{8,0},{9,1},... | collective-permute-start | bytes 1572872 | tf_op jit(solution)/shard_map/ppermute | solution.py:34
  713.1 70.8 %collective-permute-start.27 = (f32[1,1,16,8192]{3,2,1,0:T(8,128)}, f32[1,1,16,8192]{3,2,1,0:T(8,128)S(1)}, u32[]{:S(2)}, u32[]{:S(2)}) collective-permute-start(f32[1,1,16,8192]{3,2,1,0:T(8,128)} %get-tuple-element.318), channel_id=1, source_target_pairs={{0,9},{1,8},{2,11},{3,10},{4,13},{5,12},{6,15},{7,14},{8,1},{9,0},... | collective-permute-start | bytes 1572872 | tf_op jit(solution)/shard_map/ppermute | solution.py:34
  714.3 144.1 %collective-permute-start.28 = (f32[1,1,16,8192]{3,2,1,0:T(8,128)}, f32[1,1,16,8192]{3,2,1,0:T(8,128)S(1)}, u32[]{:S(2)}, u32[]{:S(2)}) collective-permute-start(f32[1,1,16,8192]{3,2,1,0:T(8,128)} %get-tuple-element.317), channel_id=1, source_target_pairs={{0,10},{1,11},{2,8},{3,9},{4,14},{5,15},{6,12},{7,13},{8,2},{9,3},... | collective-permute-start | bytes 1572872 | tf_op jit(solution)/shard_map/ppermute | solution.py:34
  762.9 120.7 %collective-permute-start.29 = (f32[1,1,16,8192]{3,2,1,0:T(8,128)}, f32[1,1,16,8192]{3,2,1,0:T(8,128)S(1)}, u32[]{:S(2)}, u32[]{:S(2)}) collective-permute-start(f32[1,1,16,8192]{3,2,1,0:T(8,128)} %get-tuple-element.316), channel_id=1, source_target_pairs={{0,11},{1,10},{2,9},{3,8},{4,15},{5,14},{6,13},{7,12},{8,3},{9,2},... | collective-permute-start | bytes 1572872 | tf_op jit(solution)/shard_map/ppermute | solution.py:34
  778.3 106.2 %collective-permute-start.30 = (f32[1,1,16,8192]{3,2,1,0:T(8,128)}, f32[1,1,16,8192]{3,2,1,0:T(8,128)S(1)}, u32[]{:S(2)}, u32[]{:S(2)}) collective-permute-start(f32[1,1,16,8192]{3,2,1,0:T(8,128)} %get-tuple-element.315), channel_id=1, source_target_pairs={{0,12},{1,13},{2,14},{3,15},{4,8},{5,9},{6,10},{7,11},{8,4},{9,5},... | collective-permute-start | bytes 1572872 | tf_op jit(solution)/shard_map/ppermute | solution.py:34
  780.6 104.7 %collective-permute-start.31 = (f32[1,1,16,8192]{3,2,1,0:T(8,128)}, f32[1,1,16,8192]{3,2,1,0:T(8,128)S(1)}, u32[]{:S(2)}, u32[]{:S(2)}) collective-permute-start(f32[1,1,16,8192]{3,2,1,0:T(8,128)} %get-tuple-element.314), channel_id=1, source_target_pairs={{0,13},{1,12},{2,15},{3,14},{4,9},{5,8},{6,11},{7,10},{8,5},{9,4},... | collective-permute-start | bytes 1572872 | tf_op jit(solution)/shard_map/ppermute | solution.py:34
  783.9 102.2 %collective-permute-start.32 = (f32[1,1,16,8192]{3,2,1,0:T(8,128)}, f32[1,1,16,8192]{3,2,1,0:T(8,128)S(1)}, u32[]{:S(2)}, u32[]{:S(2)}) collective-permute-start(f32[1,1,16,8192]{3,2,1,0:T(8,128)} %get-tuple-element.313), channel_id=1, source_target_pairs={{0,14},{1,15},{2,12},{3,13},{4,10},{5,11},{6,8},{7,9},{8,6},{9,7},... | collective-permute-start | bytes 1572872 | tf_op jit(solution)/shard_map/ppermute | solution.py:34
  858.4 28.6 %collective-permute-start.33 = (f32[1,1,16,8192]{3,2,1,0:T(8,128)}, f32[1,1,16,8192]{3,2,1,0:T(8,128)S(1)}, u32[]{:S(2)}, u32[]{:S(2)}) collective-permute-start(f32[1,1,16,8192]{3,2,1,0:T(8,128)} %get-tuple-element.312), channel_id=1, source_target_pairs={{0,15},{1,14},{2,13},{3,12},{4,11},{5,10},{6,9},{7,8},{8,7},{9,6},... | collective-permute-start | bytes 1572872 | tf_op jit(solution)/shard_map/ppermute | solution.py:34
  (14 other events, 120.2 us)
Sparse Core Ops, SparseCore 0:
  699.0 232.0 reduce-scatter.2
  985.1 101.6 reduce-scatter.4
